TPU v7x, 256 devices: a whole 4x4x8 slice. The times are simulated.
256 devices in a mesh: layer: 16 (over y_lo, z), latent: 16 (over y_hi, x, core).
Axes of the slice: x: 4, y: 4 (y_hi: 2, y_lo: 2; y = y_hi * 2 + y_lo), z: 8, core: 2. Of those that a mesh axis runs over, the one named last changes fastest.
Arguments:
- layer_inputs: bfloat16 [384, 16384], P('latent', 'layer'), may hold values from -6 to 6
- mlp_outputs: bfloat16 [384, 16384], P('latent', 'layer'), may hold values from -6 to 6
- enc_weight: bfloat16 [16384, 4096], P('layer', 'latent'), may hold values from -0.125 to 0.125
- enc_bias: float32 [8, 4096], P(None, 'latent'), may hold values from -1 to 0.5
- dec_weight: bfloat16 [8, 4096, 16384], P(None, 'latent', 'layer'), may hold values from -0.03125 to 0.03125
Outputs:
- enc_grad: float32 [16384, 4096], P('layer', 'latent')
- dec_grad: bfloat16 [8, 4096, 16384], P(None, 'latent', 'layer')
All inputs are finite; a program needn't handle non-finite values.
Results may differ from a plain program's by a relative error of at most 0.011.
Values may be sent and summed in bfloat16 or wider, within the bound.
No kernel may reach another device: no remote copies, remote signals or barrier semaphores. Data moves between devices by JAX's collectives and lax.ppermute only.
A program may use at most 64 MiB of HBM per device.

v0:
```python
import jax
import jax.numpy as jnp
from jax import lax
from jax.sharding import PartitionSpec as P


def copy_for_each(x, axis):
    copies = jnp.broadcast_to(x, (lax.axis_size(axis), *x.shape))
    return lax.all_to_all(copies, axis, split_axis=0, concat_axis=0, tiled=True)


def joined_along(parts, dim):
    parts = jnp.moveaxis(parts, 0, dim)
    dims = parts.shape
    return parts.reshape(*dims[:dim], dims[dim] * dims[dim + 1], *dims[dim + 2 :])


def gathered_copies(x, axis, dim):
    parts = copy_for_each(x, axis)
    return joined_along(parts, dim)


def from_partner(x, axis, distance):
    return lax.ppermute(x, axis, [(i, i ^ 1 << distance) for i in range(lax.axis_size(axis))])


def in_blocks(x, dim, devices):
    dims = x.shape
    parts = x.reshape(*dims[:dim], devices, dims[dim] // devices, *dims[dim + 1 :])
    return jnp.moveaxis(parts, dim, 0)


def sent_and_summed(x, axis, dim):
    parts = in_blocks(x, dim, lax.axis_size(axis))
    arrived = lax.all_to_all(parts, axis, split_axis=0, concat_axis=0, tiled=True)
    return arrived.sum(axis=0)


def take_layer(stack, index):
    return lax.dynamic_index_in_dim(stack, index, 0, keepdims=False)


def local(layer_inputs, mlp_outputs, enc_weight, enc_bias, dec_weight):
    position = lax.axis_index("layer")
    layer_now = position // 2
    which_half = position % 2
    inputs_half = gathered_copies(layer_inputs, "latent", 0)
    total_rows = inputs_half.shape[0]
    half_rows = total_rows // 2
    width_half = dec_weight.shape[2]
    latent_cols = enc_weight.shape[1]
    own_part = jnp.dot(inputs_half, enc_weight, preferred_element_type=jnp.float32)
    partner = from_partner(own_part, "layer", 0)
    pre_acts = own_part + partner + take_layer(enc_bias, layer_now)[None, :]
    latents = jnp.maximum(pre_acts, 0.0).astype(jnp.bfloat16)
    own_rows = lax.dynamic_slice_in_dim(latents, which_half * half_rows, half_rows, 0)
    gathered = gathered_copies(own_rows[None], "layer", 0)
    layer_count = gathered.shape[0] // 2
    gathered = gathered.reshape(layer_count, total_rows, latent_cols)
    upper = layer_now + 1
    rscale = total_rows ** (-0.5)
    local_rows = mlp_outputs.shape[0]

    def add_source(source, total):
        block = take_layer(gathered, source)
        return total + jnp.dot(
            block, take_layer(dec_weight, source), preferred_element_type=jnp.float32
        )

    recon_own = sent_and_summed(
        lax.fori_loop(
            0,
            upper,
            add_source,
            jnp.zeros((local_rows * lax.axis_size("latent"), width_half), jnp.float32),
        ),
        "latent",
        0,
    )
    grad_own = ((recon_own - mlp_outputs.astype(jnp.float32)) * rscale).astype(jnp.bfloat16)
    out_grad = gathered_copies(grad_own, "latent", 0)

    def back_source(source, carry):
        grads, lat_terms = carry
        block = take_layer(gathered, source)
        weight = take_layer(dec_weight, source)
        dec_piece = lax.dot_general(
            block, out_grad, (((0,), (0,)), ((), ())), preferred_element_type=jnp.float32
        ).astype(jnp.bfloat16)
        lat_piece = lax.dot_general(
            out_grad, weight, (((1,), (1,)), ((), ())), preferred_element_type=jnp.float32
        )
        grads = lax.dynamic_update_index_in_dim(grads, dec_piece, source, 0)
        lat_terms = lax.dynamic_update_index_in_dim(lat_terms, lat_piece, source, 0)
        return (grads, lat_terms)

    start_carry = (
        jnp.zeros(dec_weight.shape, jnp.bfloat16),
        jnp.zeros((layer_count, total_rows, latent_cols), jnp.float32),
    )
    dec_grad, lat_terms = lax.fori_loop(0, upper, back_source, start_carry)
    lat_all = lax.psum(lat_terms, "layer")
    lat_grad = take_layer(lat_all, layer_now)
    pre_grad = jnp.where(pre_acts > 0.0, lat_grad, 0.0).astype(jnp.bfloat16)
    enc_grad = lax.dot_general(
        inputs_half, pre_grad, (((0,), (0,)), ((), ())), preferred_element_type=jnp.float32
    )
    return (enc_grad, dec_grad)


def solution(mesh):
    in_specs = (
        P("latent", "layer"),
        P("latent", "layer"),
        P("layer", "latent"),
        P(None, "latent"),
        P(None, "latent", "layer"),
    )
    out_specs = (P("layer", "latent"), P(None, "latent", "layer"))
    return jax.shard_map(local, mesh=mesh, in_specs=in_specs, out_specs=out_specs, check_vma=False)
```

profile of v0, /device:TPU:16, one launch (start us, length us, event | category | flops | bytes accessed | tf_op | source)
XLA Modules:
  0.0 270.2 jit_solution(17720900140261801250)
XLA Ops:
  0.6 0.0 copy-start
  0.6 0.9 broadcast_in_dim.30
  1.6 19.2 %all_to_all.20 = bf16[16,24,1024]{2,1,0:T(8,128)(2,1)S(1)} all-to-all(bf16[16,24,1024]{2,1,0:T(8,128)(2,1)S(1)} %broadcast_in_dim.30), channel_id=1, replica_groups=mesh['layer'=16,'latent'=16] {'latent'}, dimensions={0} | all-to-all | bytes 1572864 | tf_op jit(solution)/shard_map/all_to_all | solution.py:9
  20.8 0.0 copy-done
  20.8 0.4 fusion.19
  21.2 2.0 collective-permute-start
  23.2 0.7 constant_dynamic-slice_fusion.1
  23.9 8.7 %collective-permute-done = f32[384,256]{1,0:T(8,128)S(1)} collective-permute-done((f32[384,256]{1,0:T(8,128)S(1)}, f32[384,256]{1,0:T(8,128)S(1)}, u32[]{:S(2)}, u32[]{:S(2)}) %collective-permute-start) | collective-permute-done | bytes 393248 | tf_op jit(solution)/shard_map/ppermute | solution.py:24
  32.6 0.1 add_add_fusion
  32.7 1.3 broadcast_in_dim.33
  33.9 9.1 %all-to-all-start.1 = ((bf16[16,1,192,256]{3,2,1,0:T(8,128)(2,1)}), bf16[16,1,192,256]{3,2,1,0:T(8,128)(2,1)S(1)}, u32[]{:S(2)}, u32[]{:S(2)}) async-start(bf16[16,1,192,256]{3,2,1,0:T(8,128)(2,1)} %broadcast_in_dim.33), calls=%async_computation.1 | async-start | bytes 3145728 | tf_op jit(solution)/shard_map/all_to_all | solution.py:9
  43.1 37.2 %all-to-all-done.1 = bf16[16,1,192,256]{3,2,1,0:T(8,128)(2,1)S(1)} async-done(((bf16[16,1,192,256]{3,2,1,0:T(8,128)(2,1)}), bf16[16,1,192,256]{3,2,1,0:T(8,128)(2,1)S(1)}, u32[]{:S(2)}, u32[]{:S(2)}) %all-to-all-start.1) | async-done | bytes 1572896 | tf_op jit(solution)/shard_map/all_to_all | solution.py:9
  80.3 0.0 copy-start.1
  80.3 1.1 copy-done.1
  81.4 0.2 broadcast_in_dim.34
  81.6 1.6 while.22
  81.6 1.6 convolution_add_fusion.2
  83.3 0.0 copy-start.2
  83.3 26.6 %all_to_all.21 = f32[16,24,1024]{2,1,0:T(8,128)} all-to-all(f32[16,24,1024]{2,1,0:T(8,128)S(1)} %bitcast.56), channel_id=1, replica_groups=mesh['layer'=16,'latent'=16] {'latent'}, dimensions={0} | all-to-all | bytes 3145728 | tf_op jit(solution)/shard_map/all_to_all | solution.py:35
  109.8 1.5 reduce_sum.9
  111.3 0.0 copy-done.2
  111.4 1.0 broadcast_in_dim.35
  112.3 6.4 %all-to-all-start.3 = ((bf16[16,24,1024]{2,1,0:T(8,128)(2,1)}), bf16[16,24,1024]{2,1,0:T(8,128)(2,1)S(1)}, u32[]{:S(2)}, u32[]{:S(2)}) async-start(bf16[16,24,1024]{2,1,0:T(8,128)(2,1)} %broadcast_in_dim.35), calls=%async_computation.3 | async-start | bytes 1572864 | tf_op jit(solution)/shard_map/all_to_all | solution.py:9
  118.8 12.3 %all-to-all-done.3 = bf16[16,24,1024]{2,1,0:T(8,128)(2,1)S(1)} async-done(((bf16[16,24,1024]{2,1,0:T(8,128)(2,1)}), bf16[16,24,1024]{2,1,0:T(8,128)(2,1)S(1)}, u32[]{:S(2)}, u32[]{:S(2)}) %all-to-all-start.3) | async-done | bytes 786464 | tf_op jit(solution)/shard_map/all_to_all | solution.py:9
  131.1 1.9 broadcast_in_dim.32
  133.0 2.5 broadcast_in_dim.31
  135.5 4.4 %while.23 = (s32[]{:T(128)}, bf16[8,256,1024]{2,1,0:T(8,128)(2,1)}, f32[8,384,256]{1,2,0:T(8,128)}, s32[]{:T(128)}, bf16[8,384,256]{2,1,0:T(8,128)(2,1)}, /*inde...) while((s32[]{:T(128)}, bf16[8,256,1024]{2,1,0:T(8,128)(2,1)}, ...), condition=%wide.region_4.5_spmd, body=%wide.region_3.4_spmd.sunk | while | flops 402915328 | bytes 3213455 | solution.py:101
  135.5 2.2 fusion.40
  137.7 2.2 fusion.39
  139.9 128.3 %all-reduce.1 = bf16[8,384,256]{1,2,0:T(8,128)(2,1)S(1)} all-reduce(f32[8,384,256]{1,2,0:T(8,128)} %get-tuple-element.70), channel_id=1, replica_groups=mesh['layer'=16,'latent'=16] {'layer'}, use_global_device_ids=true, to_apply=%region_5.6 | all-reduce | flops 786432 | bytes 4718592 | tf_op jit(solution)/shard_map/psum | solution.py:102
  268.2 0.1 copy.9
  268.4 0.5 convolution_bitcast_fusion.1
  268.8 1.3 copy.10
  (3 shorter events, 0.1 us)
Async XLA Ops:
  0.6 20.2 %copy-start = (bf16[1024,256]{1,0:T(8,128)(2,1)S(1)}, bf16[1024,256]{1,0:T(8,128)(2,1)}, u32[]{:S(2)}) copy-start(bf16[1024,256]{1,0:T(8,128)(2,1)} %param.11) | copy-start | bytes 1572868
  21.2 11.4 %collective-permute-start = (f32[384,256]{1,0:T(8,128)S(1)}, f32[384,256]{1,0:T(8,128)S(1)}, u32[]{:S(2)}, u32[]{:S(2)}) collective-permute-start(f32[384,256]{1,0:T(8,128)S(1)} %fusion.19), channel_id=1, source_target_pairs={{0,16},{16,0},{32,48},{48,32},{64,80},{80,64},{96,112},{112,96},{1... | collective-permute-start | bytes 1179656 | tf_op jit(solution)/shard_map/ppermute | solution.py:24
  33.9 46.3 %all-to-all-start.1 = ((bf16[16,1,192,256]{3,2,1,0:T(8,128)(2,1)}), bf16[16,1,192,256]{3,2,1,0:T(8,128)(2,1)S(1)}, u32[]{:S(2)}, u32[]{:S(2)}) async-start(bf16[16,1,192,256]{3,2,1,0:T(8,128)(2,1)} %broadcast_in_dim.33), calls=%async_computation.1 | async-start | bytes 3145728 | tf_op jit(solution)/shard_map/all_to_all | solution.py:9
  80.3 1.1 copy-start.1
  83.3 28.1 %copy-start.2 = (bf16[24,1024]{1,0:T(8,128)(2,1)S(1)}, bf16[24,1024]{1,0:T(8,128)(2,1)}, u32[]{:S(2)}) copy-start(bf16[24,1024]{1,0:T(8,128)(2,1)} %param.10) | copy-start | bytes 147460
  112.3 18.7 %all-to-all-start.3 = ((bf16[16,24,1024]{2,1,0:T(8,128)(2,1)}), bf16[16,24,1024]{2,1,0:T(8,128)(2,1)S(1)}, u32[]{:S(2)}, u32[]{:S(2)}) async-start(bf16[16,24,1024]{2,1,0:T(8,128)(2,1)} %broadcast_in_dim.35), calls=%async_computation.3 | async-start | bytes 1572864 | tf_op jit(solution)/shard_map/all_to_all | solution.py:9
where the time goes:
time: 271 us; the launch traced here: 270 us
  blocking collectives  174 us (64%)
  waiting for transfers between devices  58.2 us (21%)
  starting transfers between devices  17.5 us (6%)
  local copies, waits for them, and re-layouts  11.2 us (4%)
  matrix products  6.84 us (3%)
    psum x1, blocking collectives, local(): lat_all = lax.psum(lat_terms, 'layer')  128 us
    all_to_all x2, waiting for transfers between devices, copy_for_each(): return lax.all_to_all(copies, axis, split_axis=0, concat_axis=0, tiled=True)  49.5 us
    all_to_all x1, blocking collectives, sent_and_summed(): lax.all_to_all(parts, axis, split_axis=0, concat_axis=0, tiled=True)  26.6 us
    all_to_all x1, blocking collectives, copy_for_each(): return lax.all_to_all(copies, axis, split_axis=0, concat_axis=0, tiled=True)  19.2 us
    all_to_all x2, starting transfers between devices, copy_for_each(): return lax.all_to_all(copies, axis, split_axis=0, concat_axis=0, tiled=True)  15.5 us
    ppermute x1, waiting for transfers between devices, from_partner(): lax.ppermute(x, axis, [(i, i ^ 1 << distance) for i in range(lax.axis_siz...  8.69 us
  transfers between devices with their start and end apart: 3, of which 3 were waited for; matrix products, arithmetic and copies ran while one was open for 0% of the time, Pallas kernels for 0%

commit v1 on v0

--- a/solution.py
+++ b/solution.py
@@ -99,7 +99,7 @@
         jnp.zeros((layer_count, total_rows, latent_cols), jnp.float32),
     )
     dec_grad, lat_terms = lax.fori_loop(0, upper, back_source, start_carry)
-    lat_all = lax.psum(lat_terms, "layer")
+    lat_all = jnp.sum(lax.all_gather(lat_terms, "layer"), axis=0)
     lat_grad = take_layer(lat_all, layer_now)
     pre_grad = jnp.where(pre_acts > 0.0, lat_grad, 0.0).astype(jnp.bfloat16)
     enc_grad = lax.dot_general(

time: 271 us -> 740 us (2.73)
  waiting for transfers between devices: 58.2 us -> 620 us
  blocking collectives: 174 us -> 45.8 us
  other arithmetic: 1.59 us -> 20.5 us
  between operations: 0.75 us -> 14.1 us
    all_gather x0 -> x1, waiting for transfers between devices: none -> 562 us  [local(): lat_all = jnp.sum(lax.all_gather(lat_terms, 'layer'), axis=0)]
    psum x1 -> x0, blocking collectives: 128 us -> none  [local(): lat_all = lax.psum(lat_terms, 'layer')]
    reduce_sum x0 -> x1, other arithmetic: none -> 18.9 us  [local(): lat_all = jnp.sum(lax.all_gather(lat_terms, 'layer'), axis=0)]
  transfers between devices with their start and end apart: 3 -> 4, of which waited for: 3 -> 4; matrix products, arithmetic and copies ran while one was open for 0% -> 0% of each run, Pallas kernels for 0% -> 0%
where the time goes in v1:
time: 740 us; the launch traced here: 737 us
  waiting for transfers between devices  620 us (84%)
  blocking collectives  45.8 us (6%)
  other arithmetic  20.5 us (3%)
  starting transfers between devices  17.6 us (2%)
  between operations  14.1 us (2%)
  local copies, waits for them, and re-layouts  12 us (2%)
    all_gather x1, waiting for transfers between devices, local(): lat_all = jnp.sum(lax.all_gather(lat_terms, 'layer'), axis=0)  562 us
    all_to_all x2, waiting for transfers between devices, copy_for_each(): return lax.all_to_all(copies, axis, split_axis=0, concat_axis=0, tiled=True)  49.5 us
    all_to_all x1, blocking collectives, sent_and_summed(): lax.all_to_all(parts, axis, split_axis=0, concat_axis=0, tiled=True)  26.6 us
    all_to_all x1, blocking collectives, copy_for_each(): return lax.all_to_all(copies, axis, split_axis=0, concat_axis=0, tiled=True)  19.2 us
    reduce_sum x1, other arithmetic, local(): lat_all = jnp.sum(lax.all_gather(lat_terms, 'layer'), axis=0)  18.9 us
    all_to_all x2, starting transfers between devices, copy_for_each(): return lax.all_to_all(copies, axis, split_axis=0, concat_axis=0, tiled=True)  15.5 us
  transfers between devices with their start and end apart: 4, of which 4 were waited for; matrix products, arithmetic and copies ran while one was open for 0% of the time, Pallas kernels for 0%

profile of v1, /device:TPU:16, one launch (start us, length us, event | category | flops | bytes accessed | tf_op | source)
XLA Modules:
  0.0 737.4 jit_solution(3842464875461008622)
XLA Ops:
  7.2 0.0 copy-start
  7.2 0.9 broadcast_in_dim.30
  8.1 19.2 %all_to_all.20 = bf16[16,24,1024]{2,1,0:T(8,128)(2,1)S(1)} all-to-all(bf16[16,24,1024]{2,1,0:T(8,128)(2,1)S(1)} %broadcast_in_dim.30), channel_id=1, replica_groups=mesh['layer'=16,'latent'=16] {'latent'}, dimensions={0} | all-to-all | bytes 1572864 | tf_op jit(solution)/shard_map/all_to_all | solution.py:9
  27.3 0.0 copy-done
  27.3 0.4 fusion.19
  27.7 2.0 collective-permute-start
  29.7 0.7 constant_dynamic-slice_fusion
  30.4 8.7 %collective-permute-done = f32[384,256]{1,0:T(8,128)S(1)} collective-permute-done((f32[384,256]{1,0:T(8,128)S(1)}, f32[384,256]{1,0:T(8,128)S(1)}, u32[]{:S(2)}, u32[]{:S(2)}) %collective-permute-start) | collective-permute-done | bytes 393248 | tf_op jit(solution)/shard_map/ppermute | solution.py:24
  39.1 0.1 add_add_fusion
  39.2 1.3 broadcast_in_dim.33
  40.5 9.1 %all-to-all-start.1 = ((bf16[16,1,192,256]{3,2,1,0:T(8,128)(2,1)}), bf16[16,1,192,256]{3,2,1,0:T(8,128)(2,1)S(1)}, u32[]{:S(2)}, u32[]{:S(2)}) async-start(bf16[16,1,192,256]{3,2,1,0:T(8,128)(2,1)} %broadcast_in_dim.33), calls=%async_computation.1 | async-start | bytes 3145728 | tf_op jit(solution)/shard_map/all_to_all | solution.py:9
  49.6 37.2 %all-to-all-done.1 = bf16[16,1,192,256]{3,2,1,0:T(8,128)(2,1)S(1)} async-done(((bf16[16,1,192,256]{3,2,1,0:T(8,128)(2,1)}), bf16[16,1,192,256]{3,2,1,0:T(8,128)(2,1)S(1)}, u32[]{:S(2)}, u32[]{:S(2)}) %all-to-all-start.1) | async-done | bytes 1572896 | tf_op jit(solution)/shard_map/all_to_all | solution.py:9
  86.8 0.0 copy-start.2
  86.8 1.1 copy-done.2
  88.0 0.2 broadcast_in_dim.34
  88.2 1.6 while.22
  88.2 1.6 convolution_add_fusion.2
  89.8 0.0 copy-start.3
  89.8 26.6 %all_to_all.21 = f32[16,24,1024]{2,1,0:T(8,128)} all-to-all(f32[16,24,1024]{2,1,0:T(8,128)S(1)} %bitcast.55), channel_id=1, replica_groups=mesh['layer'=16,'latent'=16] {'latent'}, dimensions={0} | all-to-all | bytes 3145728 | tf_op jit(solution)/shard_map/all_to_all | solution.py:35
  116.4 1.5 reduce_sum.18
  117.9 0.0 copy-done.3
  117.9 1.0 broadcast_in_dim.35
  118.9 6.4 all-to-all-start.3
  125.3 0.0 all-gather.3.cloned.1.call-start
  125.4 12.2 %all-to-all-done.3 = bf16[16,24,1024]{2,1,0:T(8,128)(2,1)S(1)} async-done(((bf16[16,24,1024]{2,1,0:T(8,128)(2,1)}), bf16[16,24,1024]{2,1,0:T(8,128)(2,1)S(1)}, u32[]{:S(2)}, u32[]{:S(2)}) %all-to-all-start.3) | async-done | bytes 786464 | tf_op jit(solution)/shard_map/all_to_all | solution.py:9
  137.6 1.9 broadcast_in_dim.32.clone
  139.5 2.5 broadcast_in_dim.31
  142.0 4.6 while.23
  142.0 1.5 convolution_bitcast_fusion.3
  143.5 0.2 copy.19
  143.7 0.8 constant_dynamic-update-slice_fusion.2
  144.5 2.2 fusion.38
  146.7 0.0 all-gather.3.cloned.1.call-update
  146.7 562.2 %all-gather.3.cloned.1.call-done = f32[128,384,256]{2,1,0:T(8,128)} async-done(((f32[8,384,256]{2,1,0:T(8,128)}), f32[128,384,256]{2,1,0:T(8,128)}) %all-gather.3.cloned.1.call-update) | async-done | bytes 50331664 | tf_op jit(solution)/shard_map/all_gather | solution.py:102
  708.9 0.0 copy-start.1
  708.9 18.9 %reduce_sum.19 = bf16[8,384,256]{2,1,0:T(8,128)(2,1)} reduce(f32[16,8,384,256]{3,2,1,0:T(8,128)} %bitcast.56, f32[]{:T(128)} %constant.75.clone.1), dimensions={0}, to_apply=%region_5.6 | reduce | flops 11796480 | bytes 51904516 | tf_op jit(solution)/shard_map/reduce_sum | solution.py:102
  727.8 1.4 convolution_bitcast_fusion.1
  729.2 1.3 copy.11
  730.5 0.0 copy-done.1
  (2 shorter events, 0.0 us)
Async XLA Ops:
  7.2 20.2 %copy-start = (bf16[1024,256]{1,0:T(8,128)(2,1)S(1)}, bf16[1024,256]{1,0:T(8,128)(2,1)}, u32[]{:S(2)}) copy-start(bf16[1024,256]{1,0:T(8,128)(2,1)} %param.11) | copy-start | bytes 1572868
  27.7 11.4 %collective-permute-start = (f32[384,256]{1,0:T(8,128)S(1)}, f32[384,256]{1,0:T(8,128)S(1)}, u32[]{:S(2)}, u32[]{:S(2)}) collective-permute-start(f32[384,256]{1,0:T(8,128)S(1)} %fusion.19), channel_id=1, source_target_pairs={{0,16},{16,0},{32,48},{48,32},{64,80},{80,64},{96,112},{112,96},{1... | collective-permute-start | bytes 1179656 | tf_op jit(solution)/shard_map/ppermute | solution.py:24
  40.5 46.3 %all-to-all-start.1 = ((bf16[16,1,192,256]{3,2,1,0:T(8,128)(2,1)}), bf16[16,1,192,256]{3,2,1,0:T(8,128)(2,1)S(1)}, u32[]{:S(2)}, u32[]{:S(2)}) async-start(bf16[16,1,192,256]{3,2,1,0:T(8,128)(2,1)} %broadcast_in_dim.33), calls=%async_computation.1 | async-start | bytes 3145728 | tf_op jit(solution)/shard_map/all_to_all | solution.py:9
  86.8 1.1 copy-start.2
  89.8 28.1 %copy-start.3 = (bf16[24,1024]{1,0:T(8,128)(2,1)S(1)}, bf16[24,1024]{1,0:T(8,128)(2,1)}, u32[]{:S(2)}) copy-start(bf16[24,1024]{1,0:T(8,128)(2,1)} %param.10) | copy-start | bytes 147460
  118.9 18.7 %all-to-all-start.3 = ((bf16[16,24,1024]{2,1,0:T(8,128)(2,1)}), bf16[16,24,1024]{2,1,0:T(8,128)(2,1)S(1)}, u32[]{:S(2)}, u32[]{:S(2)}) async-start(bf16[16,24,1024]{2,1,0:T(8,128)(2,1)} %broadcast_in_dim.35), calls=%async_computation.3 | async-start | bytes 1572864 | tf_op jit(solution)/shard_map/all_to_all | solution.py:9
  125.3 583.6 %all-gather.3.cloned.1.call-start = ((), (), s32[]{:S(2)}) async-start(), calls=%async_computation.4 | async-start | bytes 53477376 | tf_op jit(solution)/shard_map/all_gather | solution.py:102
  708.9 21.6 %copy-start.1 = (bf16[1024,256]{1,0:T(8,128)(2,1)S(1)}, bf16[1024,256]{1,0:T(8,128)(2,1)}, u32[]{:S(2)}) copy-start(bf16[1024,256]{1,0:T(8,128)(2,1)} %param.11) | copy-start | bytes 1572868
Sparse Core Ops, SparseCore 0:
  146.8 562.0 all-gather.2
